TPU v7x, 512 devices: a whole 4x4x16 slice. The times are simulated.
512 devices in a mesh: depth: 64 (over z, x), xs: 8 (over y, core).
Axes of the slice: x: 4, y: 4, z: 16, core: 2. Of those that a mesh axis runs over, the one named last changes fastest.
Arguments:
- density: bfloat16 [1024, 128, 4096], P('depth', None, 'xs'), may hold values from 0.049804688 to 2
- clip_flags: int32 [1024, 8, 32], P('depth', None, 'xs'), may hold values 0 or 1
- band_offset: int32 [1], replicated, may hold values from 0 to 3071
- order: int32 [64], replicated, may hold values from 0 to 63, as said below
- ambient: float32 [3], replicated, may hold values from 0.1 to 0.6
- diffuse: float32 [3], replicated, may hold values from 1 to 3
Outputs:
- image: float32 [4, 128, 4096], P(None, 'depth', 'xs')
Inputs may be any that keep to these rules, and one draw needn't show every extreme that they name: The front-to-back order of a binary space partition of the slabs: order[k] = k XOR m for one m of 0 to 63.
All inputs are finite; a program needn't handle non-finite values. No bound on the sum of `clip_flags` on one device may be relied on, other than what follows from the above.
Results may differ from a plain program's by a relative error of at most 0.0003.
Values sent between devices are 32-bit elements; how exact they have to be, the bound alone decides.
A program may use at most 64 MiB of HBM per device.

v0:
```python
import math

import jax
import jax.numpy as jnp
from jax import lax
from jax.sharding import PartitionSpec as P


def laid_out(blocks, dim):
    dims = list(blocks.shape[1:])
    dims[dim] *= blocks.shape[0]
    return jnp.moveaxis(blocks, 0, dim).reshape(dims)


def sent_to_all(value, axis):
    peers = lax.axis_size(axis)
    return lax.all_to_all(
        jnp.broadcast_to(value[None], (peers, *value.shape)), axis, 0, 0, tiled=True
    )


def gathered_copies(value, axis, dim):
    return laid_out(sent_to_all(value, axis), dim)


def on_device(density, clip_flags, band_offset, order, ambient, diffuse):
    slices, rows, cells = density.shape
    depth_n = lax.axis_size("depth")
    xs_n = lax.axis_size("xs")
    kappa = 2.0 / (slices * depth_n)
    extinct = 2.0 / (cells * xs_n)
    blocks_r = clip_flags.shape[1]
    blocks_x = clip_flags.shape[2]
    full_flags = jnp.broadcast_to(
        clip_flags[:, :, None, :, None],
        (slices, blocks_r, rows // blocks_r, blocks_x, cells // blocks_x),
    )
    masked = density * full_flags.reshape(slices, rows, cells).astype(jnp.bfloat16)
    clipped = masked.astype(jnp.float32)
    upper = (
        lax.broadcasted_iota(jnp.int32, (cells, cells), 0)
        < lax.broadcasted_iota(jnp.int32, (cells, cells), 1)
    ).astype(jnp.bfloat16)
    local_prefix = jnp.dot(
        masked.reshape(slices * rows, cells), upper, preferred_element_type=jnp.float32
    ).reshape(slices, rows, cells)
    totals = jnp.sum(clipped, axis=2)
    every = gathered_copies(totals[None], "xs", 0)
    keep = (jnp.arange(xs_n, dtype=jnp.int32) < lax.axis_index("xs")).astype(jnp.float32)
    nearer = jnp.sum(every * keep[:, None, None], axis=0)
    light_depth = extinct * (nearer[:, :, None] + local_prefix)
    row_pos = (band_offset[0] + jnp.arange(rows, dtype=jnp.int32)).astype(jnp.float32)
    source = 0.6 + 0.4 * jnp.cos(2.0 * math.pi * row_pos / 64.0)
    light = source[None, :, None] * jnp.exp(-light_depth)
    before = jnp.cumsum(clipped, axis=0) - clipped
    weight = -jnp.expm1(-kappa * clipped) * jnp.exp(-kappa * before)
    base = jnp.sum(clipped * weight, axis=0)
    lit = jnp.sum(clipped * light * weight, axis=0)
    colors = ambient[:, None, None] * base[None] + diffuse[:, None, None] * lit[None]
    column = jnp.sum(clipped, axis=0)
    slab_ids = jnp.arange(depth_n, dtype=jnp.int32)
    onehot = (order[:, None] == slab_ids[None, :]).astype(jnp.int32)
    ranks = jnp.sum(onehot * slab_ids[:, None], axis=0)
    earlier = (ranks[None, :] < ranks[:, None]).astype(jnp.float32)
    stacked = jnp.concatenate([colors, column[None]], axis=0)[None]
    pieces = lax.all_to_all(stacked, "depth", split_axis=2, concat_axis=0, tiled=True)
    slab_cols = pieces[:, 3]
    front = jnp.einsum("st,tri->sri", earlier, slab_cols, precision=lax.Precision.HIGHEST)
    shaded = jnp.sum(pieces[:, :3] * jnp.exp(-kappa * front)[:, None], axis=0)
    alpha = -jnp.expm1(-kappa * jnp.sum(slab_cols, axis=0))
    return jnp.concatenate([shaded, alpha[None]], axis=0)


def solution(mesh):
    return jax.shard_map(
        on_device,
        mesh=mesh,
        in_specs=(P("depth", None, "xs"), P("depth", None, "xs"), P(), P(), P(), P()),
        out_specs=P(None, "depth", "xs"),
        check_vma=False,
    )
```

profile of v0, /device:TPU:2, one launch (start us, length us, event | category | flops | bytes accessed | tf_op | source)
XLA Modules:
  0.0 103.6 jit_solution(12383757611485044091)
XLA Ops:
  0.0 0.7 convert_element_type.27
  0.7 0.1 copy.14
  0.9 0.6 broadcast_in_dim.8
  1.5 2.2 %convert_element_type.28 = bf16[16,128,512]{2,1,0:T(8,128)(2,1)} reshape(bf16[16,8,16,4,128]{4,3,2,1,0:T(4,128)(2,1)S(1)} %broadcast_in_dim.8) | data formatting | bytes 4194304 | tf_op jit(solution)/shard_map/convert_element_type | solution.py:38
  3.7 2.9 %mul.119 = bf16[16,128,512]{2,1,0:T(8,128)(2,1)S(1)} multiply(bf16[16,128,512]{2,1,0:T(8,128)(2,1)} %param.6, bf16[16,128,512]{2,1,0:T(8,128)(2,1)} %convert_element_type.28) | non-fusion elementwise | flops 1048576 | bytes 6291456 | tf_op jit(solution)/shard_map/mul | solution.py:38
  6.7 5.0 %fusion.7 = (f32[128,512]{1,0:T(8,128)S(1)}, f32[16,128]{1,0:T(8,128)S(1)}, f32[128,512]{1,0:T(8,128)S(1)}, f32[16,128,512]{2,1,0:T(8,128)}) fusion(bf16[16,128,512]{2,1,0:T(8,128)(2,1)S(1)} %mul.119), kind=kOutput, calls=%fused_computation.13 | output fusion | flops 27129856 | bytes 6823936 | tf_op jit(solution)/shard_map/jit(cumsum)/reduce_window_sum | solution.py:55
  11.7 0.6 broadcast_in_dim.9
  12.3 4.5 %all-to-all-start = ((f32[8,1,16,128]{3,2,1,0:T(8,128)}), f32[8,1,16,128]{3,2,1,0:T(8,128)S(1)}, u32[]{:S(2)}, u32[]{:S(2)}) async-start(f32[8,1,16,128]{3,2,1,0:T(8,128)} %broadcast_in_dim.9), calls=%async_computation | async-start | bytes 131072 | tf_op jit(solution)/shard_map/all_to_all | solution.py:17
  17.5 0.2 broadcast_in_dim.10
  17.7 4.7 %all-to-all-done = f32[8,1,16,128]{3,2,1,0:T(8,128)S(1)} async-done(((f32[8,1,16,128]{3,2,1,0:T(8,128)}), f32[8,1,16,128]{3,2,1,0:T(8,128)S(1)}, u32[]{:S(2)}, u32[]{:S(2)}) %all-to-all-start) | async-done | bytes 65568 | tf_op jit(solution)/shard_map/all_to_all | solution.py:17
  22.4 0.1 fusion.18
  22.5 0.0 copy-start
  22.5 0.0 copy-start.1
  22.5 3.8 %fusion.9 = f32[128,512]{1,0:T(8,128)S(1)} fusion(f32[16,128,512]{2,1,0:T(8,128)} %get-tuple-element.8, bf16[16,128,512]{2,1,0:T(8,128)(2,1)S(1)} %mul.119, f32[16,128]{1,0:T(8,128)S(1)} %fusion.18, f32[128]{0:T(128)S(1)} %multiply_add_fusion.1), kind=kOutput, calls=%fused_computation.15 | convolution fusion | flops 1082327040 | bytes 6562304 | tf_op jit(solution)/shard_map/dot_general | solution.py:44
  26.3 0.0 copy-start.2
  26.3 0.0 copy-done
  26.3 0.0 copy-done.1
  26.3 0.3 multiply_add_fusion
  26.7 1.5 %maximum_bitcast_fusion = f32[1,4,128,512]{3,1,0,2:T(4,128)} fusion(f32[1,128,512]{2,0,1:T(1,128)S(1)} %broadcast_in_dim.10, f32[3,128,512]{2,0,1:T(4,128)S(1)} %multiply_add_fusion), kind=kLoop, calls=%fused_computation.18 | loop fusion | flops 262144 | bytes 2097152 | tf_op jit(solution)/shard_map/broadcast_in_dim | solution.py:65
  28.2 18.6 %all-to-all-start.1 = ((f32[1,4,128,512]{3,1,0,2:T(4,128)}), f32[1,4,128,512]{3,1,0,2:T(4,128)S(1)}, u32[]{:S(2)}, u32[]{:S(2)}) async-start(f32[1,4,128,512]{3,1,0,2:T(4,128)} %maximum_bitcast_fusion), calls=%async_computation.1 | async-start | bytes 2097152 | tf_op jit(solution)/shard_map/all_to_all | solution.py:66
  46.8 0.0 copy-done.2
  46.8 0.1 select_reduce_fusion
  46.9 55.0 %all-to-all-done.1 = f32[1,4,128,512]{3,1,0,2:T(4,128)S(1)} async-done(((f32[1,4,128,512]{3,1,0,2:T(4,128)}), f32[1,4,128,512]{3,1,0,2:T(4,128)S(1)}, u32[]{:S(2)}, u32[]{:S(2)}) %all-to-all-start.1) | async-done | bytes 1048608 | tf_op jit(solution)/shard_map/all_to_all | solution.py:66
  101.9 0.6 copy.17
  102.5 0.3 fusion.12
  102.9 0.1 fusion.15
  103.0 0.6 pad_maximum_fusion
  (4 shorter events, 0.1 us)
Async XLA Ops:
  12.3 10.1 %all-to-all-start = ((f32[8,1,16,128]{3,2,1,0:T(8,128)}), f32[8,1,16,128]{3,2,1,0:T(8,128)S(1)}, u32[]{:S(2)}, u32[]{:S(2)}) async-start(f32[8,1,16,128]{3,2,1,0:T(8,128)} %broadcast_in_dim.9), calls=%async_computation | async-start | bytes 131072 | tf_op jit(solution)/shard_map/all_to_all | solution.py:17
  22.5 3.8 %copy-start = (f32[3]{0:T(128)S(1)}, f32[3]{0:T(128)}, u32[]{:S(2)}) copy-start(f32[3]{0:T(128)} %param.11) | copy-start | bytes 40
  22.5 3.8 %copy-start.1 = (f32[3]{0:T(128)S(1)}, f32[3]{0:T(128)}, u32[]{:S(2)}) copy-start(f32[3]{0:T(128)} %param.10) | copy-start | bytes 40
  26.3 20.5 %copy-start.2 = (s32[64]{0:T(128)S(1)}, s32[64]{0:T(128)}, u32[]{:S(2)}) copy-start(s32[64]{0:T(128)} %param.9) | copy-start | bytes 772
  28.2 73.7 %all-to-all-start.1 = ((f32[1,4,128,512]{3,1,0,2:T(4,128)}), f32[1,4,128,512]{3,1,0,2:T(4,128)S(1)}, u32[]{:S(2)}, u32[]{:S(2)}) async-start(f32[1,4,128,512]{3,1,0,2:T(4,128)} %maximum_bitcast_fusion), calls=%async_computation.1 | async-start | bytes 2097152 | tf_op jit(solution)/shard_map/all_to_all | solution.py:66
where the time goes:
time: 104 us
  waiting for transfers between devices  59.7 us (57%)
  starting transfers between devices  23.1 us (22%)
  other arithmetic  11.5 us (11%)
  local copies, waits for them, and re-layouts  4.45 us (4%)
  matrix products  4.11 us (4%)
    all_to_all x1, waiting for transfers between devices, on_device(): lax.all_to_all(stacked, 'depth', split_axis=2, concat_axis=0, tiled=True)  55 us
    all_to_all x1, starting transfers between devices, on_device(): lax.all_to_all(stacked, 'depth', split_axis=2, concat_axis=0, tiled=True)  18.6 us
    another operation x1, other arithmetic, on_device(): before = jnp.cumsum(clipped, axis=0) - clipped  5.03 us
    all_to_all x1, waiting for transfers between devices, sent_to_all(): lax.all_to_all(jnp.broadcast_to(value[None], (peers, *value.shape)), axis...  4.73 us
    all_to_all x1, starting transfers between devices, sent_to_all(): lax.all_to_all(jnp.broadcast_to(value[None], (peers, *value.shape)), axis...  4.47 us
    dot_general x1, matrix products, on_device(): jnp.dot(masked.reshape(slices * rows, cells), upper, preferred_element_ty...  3.79 us
    mul x1, other arithmetic, on_device(): density * full_flags.reshape(slices, rows, cells).astype(jnp.bfloat16)  2.92 us
    convert_element_type x2, local copies, waits for them, and re-layouts, on_device(): full_flags.reshape(slices, rows, cells).astype(jnp.bfloat16)  2.39 us
  transfers between devices with their start and end apart: 2, of which 2 were waited for; matrix products, arithmetic and copies ran while one was open for 0% of the time, Pallas kernels for 0%

commit v1 on v0

v1 whole, which is shorter than its diff:
```python
import functools
import math

import jax
import jax.numpy as jnp
from jax import lax
from jax.experimental import pallas as pl
from jax.experimental.pallas import tpu as pltpu
from jax.sharding import PartitionSpec as P

MESH = pl.DeviceIdType.MESH
F32 = jnp.float32
BF16 = jnp.bfloat16

NZC = 16
NXC = 4
NXS = 8
NDEPTH = NZC * NXC
SZ = 16
RB = 16
XB = 128
NB = 8
CELLS = 512
EARLY = 3

HALF = (0, 1, 1, 0)
PLACE = (0, 0, 1, 1)


def xor(a, b, bits):
    total = 0
    for k in range(bits):
        p, q = (a // 2**k) % 2, (b // 2**k) % 2
        total = total + (p + q - 2 * p * q) * 2**k
    return total


def kernel(
    order_ref, off_ref, amb_ref, dif_ref, flag_ref, dens_ref, out_ref,
    dens_v, m_v, u_v, l_v, p_v, tot_v, totr_v, e_v, sbc_v, sl_v, r1bc_v, r1l_v, c1_v, r2_v, c2_v, zr_v,
    load_sem, ts_sem, tr_sem, x1bs_sem, x1br_sem, x1ls_sem, x1lr_sem, x2s_sem, x2r_sem, zs_sem, zr_sem,
    known_sem,
):
    d = lax.axis_index("depth")
    s = lax.axis_index("xs")
    z = d // NXC
    x = d % NXC
    zh, zl = z // 2, z % 2
    half = HALF_OF(x)
    place = x // 2
    kappa = 2.0 / (SZ * NDEPTH)

    def block_xor(i):
        late = i // (NB // 2)
        return late * (NB - 1 - i) + (1 - late) * (NB // 2 + i)

    def block_of(i):
        return xor(zh, block_xor(i), 3)

    def at(zz, xx):
        return (zz * NXC + xx, s)

    x1_peer = at(z, xor(x, 1, 2))
    x2_peer = at(z, xor(x, 3, 2))

    def load(i):
        return pltpu.make_async_copy(
            dens_ref.at[:, pl.ds(pl.multiple_of(block_of(i) * RB, RB), RB), :], dens_v.at[i], load_sem.at[i]
        )

    def send_tot(j):
        return pltpu.make_async_remote_copy(
            src_ref=tot_v, dst_ref=totr_v.at[j], send_sem=ts_sem.at[j], recv_sem=tr_sem.at[j],
            device_id=(d, xor(s, j, 3)), device_id_type=MESH,
        )

    def send_x1bc(i):
        return pltpu.make_async_remote_copy(
            src_ref=sbc_v.at[i, 1 - half], dst_ref=r1bc_v.at[i], send_sem=x1bs_sem.at[i], recv_sem=x1br_sem.at[i],
            device_id=x1_peer, device_id_type=MESH,
        )

    def send_x1l(i):
        return pltpu.make_async_remote_copy(
            src_ref=sl_v.at[i, 1 - half], dst_ref=r1l_v.at[i], send_sem=x1ls_sem.at[i], recv_sem=x1lr_sem.at[i],
            device_id=x1_peer, device_id_type=MESH,
        )

    def send_x2(i):
        return pltpu.make_async_remote_copy(
            src_ref=c1_v.at[i, 1 - place], dst_ref=r2_v.at[i], send_sem=x2s_sem.at[i], recv_sem=x2r_sem.at[i],
            device_id=x2_peer, device_id_type=MESH,
        )

    def send_z(i, zo):
        near = zo + zl - 2 * zo * zl
        slot = 2 * block_xor(i) + near
        return pltpu.make_async_remote_copy(
            src_ref=c2_v.at[i, zo], dst_ref=zr_v.at[slot], send_sem=zs_sem.at[slot], recv_sem=zr_sem.at[slot],
            device_id=at(2 * block_of(i) + zo, x), device_id_type=MESH,
        )

    for i in range(NB):
        load(i).start()

    barrier = pltpu.get_barrier_semaphore()
    for j in range(1, NXS):
        pl.semaphore_signal(barrier, inc=1, device_id=(d, xor(s, j, 3)), device_id_type=MESH)
    for peer in (x1_peer, x2_peer, at((z + 1) % NZC, x), at((z + NZC - 1) % NZC, x)):
        pl.semaphore_signal(barrier, inc=1, device_id=peer, device_id_type=MESH)

    def tell(k):
        step = 2**k
        for peer in (at((z + step) % NZC, x), at((z + NZC - step) % NZC, x)):
            pl.semaphore_signal(known_sem.at[k], inc=1, device_id=peer, device_id_type=MESH)

    ratio = (2.0 / (CELLS * NXS)) / kappa
    wide = CELLS // 2
    u_v[0:wide, :] = jnp.full((wide, wide), ratio, BF16)
    u_v[wide:, :] = jnp.where(
        lax.broadcasted_iota(jnp.int32, (wide, wide), 0) < lax.broadcasted_iota(jnp.int32, (wide, wide), 1), ratio, 0.0
    ).astype(BF16)

    def clip(i, carry):
        load(i).wait()
        b = block_of(i)
        for q in range(SZ):
            for c in range(CELLS // XB):
                scale = flag_ref[b, c, q].astype(F32) * (-kappa)
                cells = slice(c * XB, (c + 1) * XB)
                m_v[i, q * RB:(q + 1) * RB, cells] = (dens_v[i, q, :, cells].astype(F32) * scale).astype(BF16)
        sums = lax.dot_general(
            jnp.full((8, CELLS), ratio, BF16), m_v[i], (((1,), (1,)), ((), ())), preferred_element_type=F32
        )
        tot_v[pl.ds(i, 1), :] = sums[0:1, :]
        return carry

    lax.fori_loop(0, NB, clip, 0)

    pl.semaphore_wait(barrier, NXS + 3)
    for j in range(1, NXS):
        send_tot(j).start()
    tell(0)

    def local(i):
        m = m_v[i]
        l_v[:, 0:wide] = jnp.dot(m[:, 0:wide], u_v[wide:, :], preferred_element_type=F32)
        l_v[:, wide:] = jnp.dot(m, u_v[...], preferred_element_type=F32)
        for h in range(2):
            lanes = slice(h * wide, (h + 1) * wide)
            depth = jnp.zeros((RB, wide), F32)
            base = jnp.zeros((RB, wide), F32)
            clear = jnp.ones((RB, wide), F32)
            for q in range(SZ):
                rows = slice(q * RB, (q + 1) * RB)
                y = m_v[i, rows, lanes].astype(F32)
                depth = depth + y
                behind = jnp.exp(depth)
                term = y * (clear - behind)
                clear = behind
                base = base + term
                p_v[i, rows, lanes] = term * jnp.exp(l_v[rows, lanes])
            for g in range(8):
                zo, xx = g // 4, g % 4
                sbc_v[i, HALF[xx], PLACE[xx], zo, 0, :, lanes] = base[2 * g:2 * g + 2, :]
                sbc_v[i, HALF[xx], PLACE[xx], zo, 1, :, lanes] = depth[2 * g:2 * g + 2, :]

    def early(i, carry):
        local(i)
        send_x1bc(i).start()
        return carry

    def late(i, carry):
        local(i)
        return carry

    lax.fori_loop(0, EARLY, early, 0)
    pl.semaphore_wait(known_sem.at[0], 2)
    tell(1)
    lax.fori_loop(EARLY, NB, late, 0)

    for j in range(1, NXS):
        send_tot(j).wait_recv()
    nearer = jnp.zeros((NB, SZ * RB), F32)
    for j in range(1, NXS):
        peer = xor(s, j, 3)
        nearer = nearer + totr_v[j] * (peer < s).astype(F32)
    step = lax.broadcasted_iota(jnp.int32, (NB, SZ * RB), 0)
    lane = lax.broadcasted_iota(jnp.int32, (NB, SZ * RB), 1)
    flip = jnp.where(step < NB // 2, NB // 2 + step, NB - 1 - step)
    row = jnp.bitwise_xor(flip, zh) * RB + lane % RB + off_ref[0]
    phase = (row % 64).astype(F32) * (2.0 * math.pi / 64.0)
    factor = ((0.6 + 0.4 * jnp.cos(phase)) * jnp.exp(nearer)).T
    for i in range(NB):
        e_v[i] = jnp.broadcast_to(factor[:, i:i + 1], (SZ * RB, XB))

    pl.semaphore_wait(known_sem.at[1], 2)
    tell(2)

    def shade(i, carry):
        lit = [jnp.zeros((RB, XB), F32)] * (CELLS // XB)
        for q in range(SZ):
            rows = slice(q * RB, (q + 1) * RB)
            e = e_v[i, rows, :]
            for c in range(CELLS // XB):
                lit[c] = lit[c] + p_v[i, rows, c * XB:(c + 1) * XB] * e
        for c in range(CELLS // XB):
            for g in range(8):
                zo, xx = g // 4, g % 4
                sl_v[i, HALF[xx], PLACE[xx], zo, :, c * XB:(c + 1) * XB] = lit[c][2 * g:2 * g + 2, :]
        send_x1l(i).start()

        @pl.when(i + EARLY < NB)
        def _():
            send_x1bc(i + EARLY).start()

        return carry

    lax.fori_loop(0, NB, shade, 0)

    pl.semaphore_wait(known_sem.at[2], 2)

    mask = d ^ order_ref[0]

    def behind_if(bit):
        return ((mask // 2**bit) % 2).astype(F32)

    def over(a, b, bit):
        back = behind_if(bit)
        wa = jnp.exp(b[1] * back)
        wb = jnp.exp(a[1] * (1.0 - back))
        return a[0] * wa + b[0] * wb, a[1] + b[1], a[2] * wa + b[2] * wb

    def first(i):
        send_x1bc(i).wait_recv()
        send_x1l(i).wait_recv()
        for k in range(2):
            for zo in range(2):
                mine = (sbc_v[i, half, k, zo, 0], sbc_v[i, half, k, zo, 1], sl_v[i, half, k, zo])
                got = (r1bc_v[i, k, zo, 0], r1bc_v[i, k, zo, 1], r1l_v[i, k, zo])
                for ch, value in enumerate(over(mine, got, 0)):
                    c1_v[i, k, zo, ch] = value
        send_x2(i).start()

    def second(i):
        send_x2(i).wait_recv()
        for zo in range(2):
            mine = tuple(c1_v[i, place, zo, ch] for ch in range(3))
            got = tuple(r2_v[i, zo, ch] for ch in range(3))
            for ch, value in enumerate(over(mine, got, 1)):
                c2_v[i, zo, ch] = value

        @pl.when(i < NB - 1)
        def _():
            send_z(i, 0).start()
            send_z(i, 1).start()

        @pl.when(i == NB - 1)
        def _():
            send_z(i, 1 - zl).start()

    def swap(i, carry):
        @pl.when(i < NB)
        def _():
            first(i)

        @pl.when(i >= 2)
        def _():
            second(i - 2)

        return carry

    lax.fori_loop(0, NB + 2, swap, 0)

    def arrived(i, carry):
        send_z(i, 0).wait_recv()
        send_z(i, 1).wait_recv()
        return carry

    lax.fori_loop(0, NB - 1, arrived, 0)
    send_z(NB - 1, 1 - zl).wait_recv()

    parts = [tuple(c2_v[NB - 1, zl, ch] for ch in range(3))]
    parts += [tuple(zr_v[j, ch] for ch in range(3)) for j in range(1, NZC)]
    bit = 2
    while len(parts) > 1:
        parts = [over(parts[k], parts[k + 1], bit) for k in range(0, len(parts), 2)]
        bit += 1
    base, depth, lit = parts[0]
    for ch in range(3):
        out_ref[ch] = (amb_ref[ch] * (-1.0 / kappa)) * base + (dif_ref[ch] * (-1.0 / kappa)) * lit
    out_ref[3] = depth

    for j in range(1, NXS):
        send_tot(j).wait_send()

    def left(i, carry):
        send_x1bc(i).wait_send()
        send_x1l(i).wait_send()
        send_x2(i).wait_send()
        return carry

    lax.fori_loop(0, NB, left, 0)

    def left_z(i, carry):
        send_z(i, 0).wait_send()
        send_z(i, 1).wait_send()
        return carry

    lax.fori_loop(0, NB - 1, left_z, 0)
    send_z(NB - 1, 1 - zl).wait_send()


def HALF_OF(x):
    return ((x + 1) // 2) % 2


def on_device(density, clip_flags, band_offset, order, ambient, diffuse):
    smem = pl.BlockSpec(memory_space=pltpu.SMEM)
    dma = pltpu.SemaphoreType.DMA
    raw = pl.pallas_call(
        kernel,
        out_shape=jax.ShapeDtypeStruct((4, 2, CELLS), F32),
        in_specs=[smem, smem, smem, smem, smem, pl.BlockSpec(memory_space=pl.ANY)],
        out_specs=pl.BlockSpec(memory_space=pltpu.VMEM),
        scratch_shapes=[
            pltpu.VMEM((NB, SZ, RB, CELLS), BF16),
            pltpu.VMEM((NB, SZ * RB, CELLS), BF16),
            pltpu.VMEM((CELLS, CELLS // 2), BF16),
            pltpu.VMEM((SZ * RB, CELLS), F32),
            pltpu.VMEM((NB, SZ * RB, CELLS), F32),
            pltpu.VMEM((NB, SZ * RB), F32),
            pltpu.VMEM((NXS, NB, SZ * RB), F32),
            pltpu.VMEM((NB, SZ * RB, XB), F32),
            pltpu.VMEM((NB, 2, 2, 2, 2, 2, CELLS), F32),
            pltpu.VMEM((NB, 2, 2, 2, 2, CELLS), F32),
            pltpu.VMEM((NB, 2, 2, 2, 2, CELLS), F32),
            pltpu.VMEM((NB, 2, 2, 2, CELLS), F32),
            pltpu.VMEM((NB, 2, 2, 3, 2, CELLS), F32),
            pltpu.VMEM((NB, 2, 3, 2, CELLS), F32),
            pltpu.VMEM((NB, 2, 3, 2, CELLS), F32),
            pltpu.VMEM((NZC, 3, 2, CELLS), F32),
            dma((NB,)), dma((NXS,)), dma((NXS,)), dma((NB,)), dma((NB,)), dma((NB,)), dma((NB,)),
            dma((NB,)), dma((NB,)), dma((NZC,)), dma((NZC,)),
            pltpu.SemaphoreType.REGULAR((3,)),
        ],
        compiler_params=pltpu.CompilerParams(collective_id=0, has_side_effects=True, vmem_limit_bytes=63 * 2**20),
    )(order, band_offset, ambient, diffuse, jnp.transpose(clip_flags, (1, 2, 0)), density)
    channel = lax.broadcasted_iota(jnp.int32, raw.shape, 0)
    return jnp.where(channel == 3, -jnp.expm1(raw), raw)


def solution(mesh):
    return jax.shard_map(
        on_device,
        mesh=mesh,
        in_specs=(P("depth", None, "xs"), P("depth", None, "xs"), P(), P(), P(), P()),
        out_specs=P(None, "depth", "xs"),
        check_vma=False,
    )
```

time: 104 us -> 40.9 us (0.39)
  the two profiles are of different devices: /device:TPU:2 before, /device:TPU:1 now
where the time goes in v1:
time: 40.9 us; the launch traced here: 40.6 us
  Pallas kernels  38.6 us (94%)
  other arithmetic  1.4 us (3%)
  between operations  0.67 us (2%)
    pallas_call x1, Pallas kernels, on_device(): pl.pallas_call(kernel, out_shape=jax.ShapeDtypeStruct((4, 2, CELLS), F32)...  38.6 us
    select_n x1, other arithmetic, on_device(): return jnp.where(channel == 3, -jnp.expm1(raw), raw)  1.4 us

profile of v1, /device:TPU:1, one launch (start us, length us, event | category | flops | bytes accessed | tf_op | source)
XLA Modules:
  0.0 40.6 jit_solution(9919034698349712247)
XLA Ops:
  0.7 38.6 %shard_map.64 = f32[4,2,512]{2,1,0:T(2,128)} custom-call(s32[64]{0:T(128)} %order_ref.1, s32[1]{0:T(128)S(6)} %copy.7.off_ref, f32[3]{0:T(128)} %amb_ref.1, f32[3]{0:T(128)} %dif_ref.1, s32[8,4,16]{2,1,0:T(4,128)} %bitcast.1, bf16[16,128,512]{2,1,0:T(8,128)(2,1)} %dens_ref.1), custom_call_target="tpu_custom_call" | custom-call | tf_op jit(solution)/shard_map/pallas_call | solution.py:321
  39.2 1.4 %negate_select_fusion = f32[4,2,512]{2,1,0:T(2,128)} fusion(f32[4,2,512]{2,1,0:T(2,128)} %shard_map.64, pred[4]{0:T(512)(128)(4,1)S(1)} %iota_compare_fusion), kind=kLoop, calls=%fused_computation | loop fusion | flops 8192 | bytes 32772 | tf_op jit(solution)/shard_map/jit(_where)/select_n | solution.py:350
  (1 shorter events, 0.0 us)

commit v2 on v1

v2 whole, which is shorter than its diff:
```python
import functools
import math

import jax
import jax.numpy as jnp
from jax import lax
from jax.experimental import pallas as pl
from jax.experimental.pallas import tpu as pltpu
from jax.sharding import PartitionSpec as P

MESH = pl.DeviceIdType.MESH
F32 = jnp.float32
BF16 = jnp.bfloat16

NZC = 16
NXC = 4
NXS = 8
NDEPTH = NZC * NXC
SZ = 16
RB = 16
XB = 128
NB = 8
CELLS = 512

HALF = (0, 1, 1, 0)
PLACE = (0, 0, 1, 1)


def xor(a, b, bits):
    total = 0
    for k in range(bits):
        p, q = (a // 2**k) % 2, (b // 2**k) % 2
        total = total + (p + q - 2 * p * q) * 2**k
    return total


def kernel(
    order_hbm, off_hbm, amb_hbm, dif_hbm, flag_hbm, dens_ref, out_ref,
    order_ref, off_ref, amb_ref, dif_ref, flag_ref,
    dens_v, m_v, u_v, l_v, p_v, tot_v, totr_v, e_v, sbc_v, sl_v, r1bc_v, r1l_v, c1bc_v, c1l_v, r2bc_v, r2l_v,
    c2bc_v, c2l_v, r3bc_v, r3l_v, c3bc_v, c3l_v, zbc_v, zl_v,
    small_sem, load_sem, ts_sem, tr_sem, send_sem, recv_sem, known_sem,
):
    d = lax.axis_index("depth")
    s = lax.axis_index("xs")
    z = d // NXC
    x = d % NXC
    zh, zl = z // 2, z % 2
    half = HALF_OF(x)
    place = x // 2
    kappa = 2.0 / (SZ * NDEPTH)

    def block_xor(i):
        late = i // (NB // 2)
        return late * (NB - 1 - i) + (1 - late) * (NB // 2 + i)

    def block_of(i):
        return xor(zh, block_xor(i), 3)

    def at(zz, xx):
        return (zz * NXC + xx, s)

    x1_peer = at(z, xor(x, 1, 2))
    x2_peer = at(z, xor(x, 3, 2))
    z1_peer = at(z + 1 - 2 * zl, x)

    def load(i):
        return pltpu.make_async_copy(
            dens_ref.at[:, pl.ds(pl.multiple_of(block_of(i) * RB, RB), RB), :], dens_v.at[i], load_sem.at[i]
        )

    small = [
        pltpu.make_async_copy(source, target, small_sem.at[k])
        for k, (source, target) in enumerate((
            (flag_hbm, flag_ref), (order_hbm, order_ref), (off_hbm, off_ref), (amb_hbm, amb_ref), (dif_hbm, dif_ref),
        ))
    ]

    def send_tot(j):
        return pltpu.make_async_remote_copy(
            src_ref=tot_v, dst_ref=totr_v.at[j], send_sem=ts_sem.at[j], recv_sem=tr_sem.at[j],
            device_id=(d, xor(s, j, 3)), device_id_type=MESH,
        )

    def send(stage, source, target, i, peer):
        return pltpu.make_async_remote_copy(
            src_ref=source, dst_ref=target, send_sem=send_sem.at[stage, i], recv_sem=recv_sem.at[stage, i],
            device_id=peer, device_id_type=MESH,
        )

    def x1bc(i):
        return send(0, sbc_v.at[i, 1 - half], r1bc_v.at[i], i, x1_peer)

    def x1l(i):
        return send(1, sl_v.at[i, 1 - half], r1l_v.at[i], i, x1_peer)

    def x2bc(i):
        return send(2, c1bc_v.at[i, 1 - place], r2bc_v.at[i], i, x2_peer)

    def x2l(i):
        return send(3, c1l_v.at[i, 1 - place], r2l_v.at[i], i, x2_peer)

    def z1bc(i):
        return send(4, c2bc_v.at[i, 1 - zl], r3bc_v.at[i], i, z1_peer)

    def z1l(i):
        return send(5, c2l_v.at[i, 1 - zl], r3l_v.at[i], i, z1_peer)

    def farbc(i):
        return send(6, c3bc_v.at[i], zbc_v.at[i], i, at(2 * block_of(i) + zl, x))

    def farl(i):
        return send(7, c3l_v.at[i], zl_v.at[i], i, at(2 * block_of(i) + zl, x))

    small[0].start()
    for i in range(NB):
        load(i).start()
    for copy in small[1:]:
        copy.start()

    barrier = pltpu.get_barrier_semaphore()
    for j in range(1, NXS):
        pl.semaphore_signal(barrier, inc=1, device_id=(d, xor(s, j, 3)), device_id_type=MESH)
    for peer in (x1_peer, x2_peer, at((z + 1) % NZC, x), at((z + NZC - 1) % NZC, x)):
        pl.semaphore_signal(barrier, inc=1, device_id=peer, device_id_type=MESH)

    def tell(k):
        step = 2**k
        for peer in (at((z + step) % NZC, x), at((z + NZC - step) % NZC, x)):
            pl.semaphore_signal(known_sem.at[k], inc=1, device_id=peer, device_id_type=MESH)

    ratio = (2.0 / (CELLS * NXS)) / kappa
    wide = CELLS // 2
    u_v[0:wide, :] = jnp.full((wide, wide), ratio, BF16)
    u_v[wide:, :] = jnp.where(
        lax.broadcasted_iota(jnp.int32, (wide, wide), 0) < lax.broadcasted_iota(jnp.int32, (wide, wide), 1), ratio, 0.0
    ).astype(BF16)

    def clip(i):
        load(i).wait()
        b = block_of(i)
        for q in range(SZ):
            for c in range(CELLS // XB):
                scale = flag_ref[b, c, q].astype(F32) * (-kappa)
                cells = slice(c * XB, (c + 1) * XB)
                m_v[i, q * RB:(q + 1) * RB, cells] = (dens_v[i, q, :, cells].astype(F32) * scale).astype(BF16)
        sums = lax.dot_general(
            jnp.full((8, CELLS), ratio, BF16), m_v[i], (((1,), (1,)), ((), ())), preferred_element_type=F32
        )
        tot_v[pl.ds(i, 1), :] = sums[0:1, :]

    def local(i):
        m = m_v[i]
        l_v[:, 0:wide] = jnp.dot(m[:, 0:wide], u_v[wide:, :], preferred_element_type=F32)
        l_v[:, wide:] = jnp.dot(m, u_v[...], preferred_element_type=F32)
        for h in range(2):
            lanes = slice(h * wide, (h + 1) * wide)
            depth = jnp.zeros((RB, wide), F32)
            base = jnp.zeros((RB, wide), F32)
            clear = jnp.ones((RB, wide), F32)
            for q in range(SZ):
                rows = slice(q * RB, (q + 1) * RB)
                y = m_v[i, rows, lanes].astype(F32)
                depth = depth + y
                behind = jnp.exp(depth)
                term = y * (clear - behind)
                clear = behind
                base = base + term
                p_v[i, rows, lanes] = term * jnp.exp(l_v[rows, lanes])
            for g in range(8):
                zo, xx = g // 4, g % 4
                sbc_v[i, HALF[xx], PLACE[xx], zo, 0, :, lanes] = base[2 * g:2 * g + 2, :]
                sbc_v[i, HALF[xx], PLACE[xx], zo, 1, :, lanes] = depth[2 * g:2 * g + 2, :]

    def back_of(bit):
        return (((d ^ order_ref[0]) // 2**bit) % 2).astype(F32)

    def weights(mine, got, back):
        return jnp.exp(got * back), jnp.exp(mine * (1.0 - back))

    def when(start, stop, t):
        return pl.when(jnp.logical_and(t >= start, t < stop))

    def first_bc(i):
        x1bc(i).wait_recv()
        back = back_of(0)
        for k in range(2):
            for zo in range(2):
                mine, got = sbc_v[i, half, k, zo, 1], r1bc_v[i, k, zo, 1]
                wa, wb = weights(mine, got, back)
                c1bc_v[i, k, zo, 0] = sbc_v[i, half, k, zo, 0] * wa + r1bc_v[i, k, zo, 0] * wb
                c1bc_v[i, k, zo, 1] = mine + got
        x2bc(i).start()

    def first_l(i):
        x1l(i).wait_recv()
        back = back_of(0)
        for k in range(2):
            for zo in range(2):
                wa, wb = weights(sbc_v[i, half, k, zo, 1], r1bc_v[i, k, zo, 1], back)
                c1l_v[i, k, zo] = sl_v[i, half, k, zo] * wa + r1l_v[i, k, zo] * wb
        x2l(i).start()

    def second_bc(i):
        x2bc(i).wait_recv()
        back = back_of(1)
        for zo in range(2):
            mine, got = c1bc_v[i, place, zo, 1], r2bc_v[i, zo, 1]
            wa, wb = weights(mine, got, back)
            c2bc_v[i, zo, 0] = c1bc_v[i, place, zo, 0] * wa + r2bc_v[i, zo, 0] * wb
            c2bc_v[i, zo, 1] = mine + got
        z1bc(i).start()

    def second_l(i):
        x2l(i).wait_recv()
        back = back_of(1)
        for zo in range(2):
            wa, wb = weights(c1bc_v[i, place, zo, 1], r2bc_v[i, zo, 1], back)
            c2l_v[i, zo] = c1l_v[i, place, zo] * wa + r2l_v[i, zo] * wb
        z1l(i).start()

    def third_bc(i):
        z1bc(i).wait_recv()
        mine, got = c2bc_v[i, zl, 1], r3bc_v[i, 1]
        wa, wb = weights(mine, got, back_of(2))
        c3bc_v[i, 0] = c2bc_v[i, zl, 0] * wa + r3bc_v[i, 0] * wb
        c3bc_v[i, 1] = mine + got

        @pl.when(i < NB - 1)
        def _():
            farbc(i).start()

    def third_l(i):
        z1l(i).wait_recv()
        wa, wb = weights(c2bc_v[i, zl, 1], r3bc_v[i, 1], back_of(2))
        c3l_v[i] = c2l_v[i, zl] * wa + r3l_v[i] * wb

        @pl.when(i < NB - 1)
        def _():
            farl(i).start()

    small[0].wait()
    clip(0)
    local(0)
    pl.semaphore_wait(barrier, NXS + 3)
    x1bc(0).start()
    tell(0)
    for copy in small[1:]:
        copy.wait()

    def produce(t, carry):
        @pl.when(t == 1)
        def _():
            clip(1)

        local(t)
        x1bc(t).start()

        @pl.when(t == 1)
        def _():
            pl.semaphore_wait(known_sem.at[0], 2)
            tell(1)

            def rest(i, inner):
                clip(i)
                return inner

            lax.fori_loop(2, NB, rest, 0)
            for j in range(1, NXS):
                send_tot(j).start()

        @pl.when(t == 3)
        def _():
            pl.semaphore_wait(known_sem.at[1], 2)
            tell(2)

        @when(3, NB, t)
        def _():
            first_bc(t - 3)

        @when(6, NB, t)
        def _():
            second_bc(t - 6)

        return carry

    lax.fori_loop(1, NB, produce, 0)

    for j in range(1, NXS):
        send_tot(j).wait_recv()
    nearer = jnp.zeros((NB, SZ * RB), F32)
    for j in range(1, NXS):
        peer = xor(s, j, 3)
        nearer = nearer + totr_v[j] * (peer < s).astype(F32)
    step = lax.broadcasted_iota(jnp.int32, (NB, SZ * RB), 0)
    lane = lax.broadcasted_iota(jnp.int32, (NB, SZ * RB), 1)
    flip = jnp.where(step < NB // 2, NB // 2 + step, NB - 1 - step)
    row = jnp.bitwise_xor(flip, zh) * RB + lane % RB + off_ref[0]
    phase = (row % 64).astype(F32) * (2.0 * math.pi / 64.0)
    factor = ((0.6 + 0.4 * jnp.cos(phase)) * jnp.exp(nearer)).T
    for i in range(NB):
        e_v[i] = jnp.broadcast_to(factor[:, i:i + 1], (SZ * RB, XB))

    def shade(i, carry):
        lit = [jnp.zeros((RB, XB), F32)] * (CELLS // XB)
        for q in range(SZ):
            rows = slice(q * RB, (q + 1) * RB)
            e = e_v[i, rows, :]
            for c in range(CELLS // XB):
                lit[c] = lit[c] + p_v[i, rows, c * XB:(c + 1) * XB] * e
        for c in range(CELLS // XB):
            for g in range(8):
                zo, xx = g // 4, g % 4
                sl_v[i, HALF[xx], PLACE[xx], zo, :, c * XB:(c + 1) * XB] = lit[c][2 * g:2 * g + 2, :]
        x1l(i).start()
        return carry

    lax.fori_loop(0, NB, shade, 0)

    def early(i, carry):
        second_bc(i)
        return carry

    lax.fori_loop(2, 5, early, 0)
    pl.semaphore_wait(known_sem.at[2], 2)

    def swap(t, carry):
        @when(0, 3, t)
        def _():
            first_bc(t + 5)

        @when(3, 11, t)
        def _():
            third_bc(t - 3)

        @when(3, 11, t)
        def _():
            first_l(t - 3)

        @when(3, 6, t)
        def _():
            second_bc(t + 2)

        @when(7, 15, t)
        def _():
            second_l(t - 7)

        @when(11, 19, t)
        def _():
            third_l(t - 11)

        return carry

    lax.fori_loop(0, 19, swap, 0)

    def arrived(i, carry):
        farbc(i).wait_recv()
        farl(i).wait_recv()
        return carry

    lax.fori_loop(0, NB - 1, arrived, 0)

    own = (c3bc_v[NB - 1, 0], c3bc_v[NB - 1, 1], c3l_v[NB - 1])
    parts = [own] + [None] * (NB - 1)
    for i in range(NB - 1):
        parts[block_xor(i)] = (zbc_v[i, 0], zbc_v[i, 1], zl_v[i])
    bit = 3
    while len(parts) > 1:
        back = back_of(bit)
        joined = []
        for a, b in zip(parts[0::2], parts[1::2], strict=True):
            wa, wb = weights(a[1], b[1], back)
            joined.append((a[0] * wa + b[0] * wb, a[1] + b[1], a[2] * wa + b[2] * wb))
        parts = joined
        bit += 1
    base, depth, lit = parts[0]
    for ch in range(3):
        out_ref[ch] = (amb_ref[ch] * (-1.0 / kappa)) * base + (dif_ref[ch] * (-1.0 / kappa)) * lit
    out_ref[3] = depth

    for j in range(1, NXS):
        send_tot(j).wait_send()

    def left(i, carry):
        for copy in (x1bc(i), x1l(i), x2bc(i), x2l(i), z1bc(i), z1l(i)):
            copy.wait_send()
        return carry

    lax.fori_loop(0, NB, left, 0)

    def left_far(i, carry):
        farbc(i).wait_send()
        farl(i).wait_send()
        return carry

    lax.fori_loop(0, NB - 1, left_far, 0)


def HALF_OF(x):
    return ((x + 1) // 2) % 2


def on_device(density, clip_flags, band_offset, order, ambient, diffuse):
    hbm = pl.BlockSpec(memory_space=pltpu.HBM)
    dma = pltpu.SemaphoreType.DMA
    flags = jnp.transpose(clip_flags, (1, 2, 0))
    bc = (2, 2, CELLS)
    raw = pl.pallas_call(
        kernel,
        out_shape=jax.ShapeDtypeStruct((4, 2, CELLS), F32),
        in_specs=[hbm] * 6,
        out_specs=pl.BlockSpec(memory_space=pltpu.VMEM),
        scratch_shapes=[
            pltpu.SMEM(order.shape, order.dtype),
            pltpu.SMEM(band_offset.shape, band_offset.dtype),
            pltpu.SMEM(ambient.shape, ambient.dtype),
            pltpu.SMEM(diffuse.shape, diffuse.dtype),
            pltpu.SMEM(flags.shape, flags.dtype),
            pltpu.VMEM((NB, SZ, RB, CELLS), BF16),
            pltpu.VMEM((NB, SZ * RB, CELLS), BF16),
            pltpu.VMEM((CELLS, CELLS // 2), BF16),
            pltpu.VMEM((SZ * RB, CELLS), F32),
            pltpu.VMEM((NB, SZ * RB, CELLS), F32),
            pltpu.VMEM((NB, SZ * RB), F32),
            pltpu.VMEM((NXS, NB, SZ * RB), F32),
            pltpu.VMEM((NB, SZ * RB, XB), F32),
            pltpu.VMEM((NB, 2, 2, 2) + bc, F32),
            pltpu.VMEM((NB, 2, 2, 2, 2, CELLS), F32),
            pltpu.VMEM((NB, 2, 2) + bc, F32),
            pltpu.VMEM((NB, 2, 2, 2, CELLS), F32),
            pltpu.VMEM((NB, 2, 2) + bc, F32),
            pltpu.VMEM((NB, 2, 2, 2, CELLS), F32),
            pltpu.VMEM((NB, 2) + bc, F32),
            pltpu.VMEM((NB, 2, 2, CELLS), F32),
            pltpu.VMEM((NB, 2) + bc, F32),
            pltpu.VMEM((NB, 2, 2, CELLS), F32),
            pltpu.VMEM((NB,) + bc, F32),
            pltpu.VMEM((NB, 2, CELLS), F32),
            pltpu.VMEM((NB,) + bc, F32),
            pltpu.VMEM((NB, 2, CELLS), F32),
            pltpu.VMEM((NB,) + bc, F32),
            pltpu.VMEM((NB, 2, CELLS), F32),
            dma((5,)), dma((NB,)), dma((NXS,)), dma((NXS,)), dma((8, NB)), dma((8, NB)),
            pltpu.SemaphoreType.REGULAR((3,)),
        ],
        compiler_params=pltpu.CompilerParams(collective_id=0, has_side_effects=True, vmem_limit_bytes=63 * 2**20),
    )(order, band_offset, ambient, diffuse, flags, density)
    channel = lax.broadcasted_iota(jnp.int32, raw.shape, 0)
    return jnp.where(channel == 3, -jnp.expm1(raw), raw)


def solution(mesh):
    return jax.shard_map(
        on_device,
        mesh=mesh,
        in_specs=(P("depth", None, "xs"), P("depth", None, "xs"), P(), P(), P(), P()),
        out_specs=P(None, "depth", "xs"),
        check_vma=False,
    )
```

time: 40.9 us -> 44 us (1.076)
  the two profiles are of different devices: /device:TPU:1 before, /device:TPU:32 now
where the time goes in v2:
time: 44 us; the launch traced here: 43.8 us
  Pallas kernels  41.7 us (95%)
  other arithmetic  1.4 us (3%)
  between operations  0.67 us (2%)
    pallas_call x1, Pallas kernels, on_device(): pl.pallas_call(kernel, out_shape=jax.ShapeDtypeStruct((4, 2, CELLS), F32)...  41.7 us
    select_n x1, other arithmetic, on_device(): return jnp.where(channel == 3, -jnp.expm1(raw), raw)  1.4 us

profile of v2, /device:TPU:32, one launch (start us, length us, event | category | flops | bytes accessed | tf_op | source)
XLA Modules:
  0.0 43.8 jit_solution(6702732130693669427)
XLA Ops:
  0.7 41.7 %shard_map.64 = f32[4,2,512]{2,1,0:T(2,128)} custom-call(s32[64]{0:T(128)} %order_hbm.1, s32[1]{0:T(128)S(6)} %copy.7.off_hbm, f32[3]{0:T(128)} %amb_hbm.1, f32[3]{0:T(128)} %dif_hbm.1, s32[8,4,16]{2,1,0:T(4,128)} %bitcast.1, bf16[16,128,512]{2,1,0:T(8,128)(2,1)} %dens_ref.1), custom_call_target="tpu_custom_call" | custom-call | tf_op jit(solution)/shard_map/pallas_call | solution.py:408
  42.4 1.4 %negate_select_fusion = f32[4,2,512]{2,1,0:T(2,128)} fusion(f32[4,2,512]{2,1,0:T(2,128)} %shard_map.64, pred[4]{0:T(512)(128)(4,1)S(1)} %iota_compare_fusion), kind=kLoop, calls=%fused_computation | loop fusion | flops 8192 | bytes 32772 | tf_op jit(solution)/shard_map/jit(_where)/select_n | solution.py:449
  (1 shorter events, 0.0 us)

commit v3 on v1

v3 whole, which is shorter than its diff:
```python
import functools
import math

import jax
import jax.numpy as jnp
from jax import lax
from jax.experimental import pallas as pl
from jax.experimental.pallas import tpu as pltpu
from jax.sharding import PartitionSpec as P

MESH = pl.DeviceIdType.MESH
F32 = jnp.float32
BF16 = jnp.bfloat16

NZC = 16
NXC = 4
NXS = 8
NDEPTH = NZC * NXC
SZ = 16
RB = 16
XB = 128
NB = 8
CELLS = 512

EARLY = 5


def xor(a, b, bits):
    total = 0
    for k in range(bits):
        p, q = (a // 2**k) % 2, (b // 2**k) % 2
        total = total + (p + q - 2 * p * q) * 2**k
    return total


def kernel(
    order_hbm, off_hbm, amb_hbm, dif_hbm, flag_hbm, dens_ref, out_ref,
    order_ref, off_ref, amb_ref, dif_ref, flag_ref,
    dens_v, m_v, u_v, l_v, p_v, tot_v, totr_v, e_v, sbc_v, sl_v, rbc_v, rl_v, cbc_v, cl_v, zbc_v, zl_v,
    small_sem, load_sem, ts_sem, tr_sem, xs_sem, xr_sem, zs_sem, zr_sem, known_sem,
):
    d = lax.axis_index("depth")
    s = lax.axis_index("xs")
    z = d // NXC
    x = d % NXC
    zh, zl = z // 2, z % 2
    kappa = 2.0 / (SZ * NDEPTH)

    def block_of(i):
        return (zh + NB // 2 + ((i + 1) // 2) * (1 - 2 * (i % 2))) % NB

    def at(zz, xx):
        return (zz * NXC + xx, s)

    def load(i):
        return pltpu.make_async_copy(
            dens_ref.at[:, pl.ds(pl.multiple_of(block_of(i) * RB, RB), RB), :], dens_v.at[i], load_sem.at[i]
        )

    small = [
        pltpu.make_async_copy(source, target, small_sem.at[k])
        for k, (source, target) in enumerate((
            (flag_hbm, flag_ref), (order_hbm, order_ref), (off_hbm, off_ref), (amb_hbm, amb_ref), (dif_hbm, dif_ref),
        ))
    ]

    def send_tot(j):
        return pltpu.make_async_remote_copy(
            src_ref=tot_v, dst_ref=totr_v.at[j], send_sem=ts_sem.at[j], recv_sem=tr_sem.at[j],
            device_id=(d, xor(s, j, 3)), device_id_type=MESH,
        )

    def send_x(kind, i, j):
        source, target = ((sbc_v, rbc_v), (sl_v, rl_v))[kind]
        peer = xor(x, j, 2)
        return pltpu.make_async_remote_copy(
            src_ref=source.at[i, peer], dst_ref=target.at[i, j - 1],
            send_sem=xs_sem.at[kind, i, j - 1], recv_sem=xr_sem.at[kind, i, j - 1],
            device_id=at(z, peer), device_id_type=MESH,
        )

    def send_z(kind, i, zo):
        source, target = ((cbc_v, zbc_v), (cl_v, zl_v))[kind]
        return pltpu.make_async_remote_copy(
            src_ref=source.at[i, zo], dst_ref=target.at[z],
            send_sem=zs_sem.at[kind, i, zo], recv_sem=zr_sem.at[kind, z],
            device_id=at(2 * block_of(i) + zo, x), device_id_type=MESH,
        )

    def from_z(kind, k):
        source, target = ((cbc_v, zbc_v), (cl_v, zl_v))[kind]
        peer = (z + k) % NZC
        return pltpu.make_async_remote_copy(
            src_ref=source.at[0, 0], dst_ref=target.at[peer],
            send_sem=zs_sem.at[kind, 0, 0], recv_sem=zr_sem.at[kind, peer],
            device_id=at(peer, x), device_id_type=MESH,
        )

    small[0].start()
    for i in range(NB):
        load(i).start()
    barrier = pltpu.get_barrier_semaphore()
    for j in range(1, NXS):
        pl.semaphore_signal(barrier, inc=1, device_id=(d, xor(s, j, 3)), device_id_type=MESH)
    for j in range(1, NXC):
        pl.semaphore_signal(barrier, inc=1, device_id=at(z, xor(x, j, 2)), device_id_type=MESH)
    for step in (1, NZC - 1):
        pl.semaphore_signal(barrier, inc=1, device_id=at((z + step) % NZC, x), device_id_type=MESH)
    for copy in small[1:]:
        copy.start()

    def tell(k):
        for step in (2**k, NZC - 2**k):
            pl.semaphore_signal(
                known_sem.at[k], inc=1, device_id=at((z + step) % NZC, x), device_id_type=MESH
            )

    ratio = (2.0 / (CELLS * NXS)) / kappa
    wide = CELLS // 2
    u_v[0:wide, :] = jnp.full((wide, wide), ratio, BF16)
    u_v[wide:, :] = jnp.where(
        lax.broadcasted_iota(jnp.int32, (wide, wide), 0) < lax.broadcasted_iota(jnp.int32, (wide, wide), 1), ratio, 0.0
    ).astype(BF16)

    pl.semaphore_wait(barrier, NXS - 1 + NXC - 1 + 2)
    tell(0)

    small[0].wait()

    def clip(i, carry):
        load(i).wait()
        b = block_of(i)
        for q in range(SZ):
            for c in range(CELLS // XB):
                scale = flag_ref[b, c, q].astype(F32) * (-kappa)
                cells = slice(c * XB, (c + 1) * XB)
                m_v[i, q * RB:(q + 1) * RB, cells] = (dens_v[i, q, :, cells].astype(F32) * scale).astype(BF16)
        return carry

    lax.fori_loop(0, NB, clip, 0)

    ones = jnp.full((8, CELLS), ratio, BF16)
    for i in range(NB):
        sums = lax.dot_general(ones, m_v[i], (((1,), (1,)), ((), ())), preferred_element_type=F32)
        tot_v[i:i + 1, :] = sums[0:1, :]
    for j in range(1, NXS):
        send_tot(j).start()
    pl.semaphore_wait(known_sem.at[0], 2)
    tell(1)

    def local(i):
        m = m_v[i]
        l_v[:, 0:wide] = jnp.dot(m[:, 0:wide], u_v[wide:, :], preferred_element_type=F32)
        l_v[:, wide:] = jnp.dot(m, u_v[...], preferred_element_type=F32)
        for h in range(2):
            lanes = slice(h * wide, (h + 1) * wide)
            depth = jnp.zeros((RB, wide), F32)
            base = jnp.zeros((RB, wide), F32)
            clear = jnp.ones((RB, wide), F32)
            for q in range(SZ):
                rows = slice(q * RB, (q + 1) * RB)
                y = m_v[i, rows, lanes].astype(F32)
                depth = depth + y
                behind = jnp.exp(depth)
                term = y * (clear - behind)
                clear = behind
                base = base + term
                p_v[i, rows, lanes] = term * jnp.exp(l_v[rows, lanes])
            for g in range(8):
                sbc_v[i, g % 4, g // 4, 0, :, lanes] = base[2 * g:2 * g + 2, :]
                sbc_v[i, g % 4, g // 4, 1, :, lanes] = depth[2 * g:2 * g + 2, :]

    def produce(i, carry):
        local(i)

        @pl.when(i < EARLY)
        def _():
            for j in range(1, NXC):
                send_x(0, i, j).start()

        @pl.when(i == NB // 2)
        def _():
            pl.semaphore_wait(known_sem.at[1], 2)
            tell(2)

        return carry

    lax.fori_loop(0, NB, produce, 0)

    for copy in small[1:]:
        copy.wait()
    row = lax.broadcasted_iota(jnp.int32, (2, CELLS), 0) + (2 * d + off_ref[0])
    source = 0.6 + 0.4 * jnp.cos((row % 64).astype(F32) * (2.0 * math.pi / 64.0))

    for j in range(1, NXS):
        send_tot(j).wait_recv()
    nearer = jnp.zeros((NB, SZ * RB), F32)
    for j in range(1, NXS):
        nearer = nearer + totr_v[j] * (xor(s, j, 3) < s).astype(F32)
    factor = jnp.exp(nearer).T
    for i in range(NB):
        e_v[i] = jnp.broadcast_to(factor[:, i:i + 1], (SZ * RB, XB))

    def shade(i, carry):
        lit = [jnp.zeros((RB, XB), F32)] * (CELLS // XB)
        for q in range(SZ):
            rows = slice(q * RB, (q + 1) * RB)
            e = e_v[i, rows, :]
            for c in range(CELLS // XB):
                lit[c] = lit[c] + p_v[i, rows, c * XB:(c + 1) * XB] * e
        for c in range(CELLS // XB):
            for g in range(8):
                sl_v[i, g % 4, g // 4, :, c * XB:(c + 1) * XB] = lit[c][2 * g:2 * g + 2, :]
        for j in range(1, NXC):
            send_x(1, i, j).start()

        @pl.when(i < NB - EARLY)
        def _():
            for j in range(1, NXC):
                send_x(0, i + EARLY, j).start()

        return carry

    lax.fori_loop(0, NB, shade, 0)

    def back_of(rank, bit):
        return ((rank // 2**bit) % 2).astype(F32)

    def weights(a, b, back):
        return jnp.exp(b * back), jnp.exp(a * (1.0 - back))

    rank = d ^ order_ref[0]

    def columns(i, zo):
        return [sbc_v[i, x, zo, 1]] + [rbc_v[i, j, zo, 1] for j in range(3)]

    def shares(cols):
        w0, w1 = weights(cols[0], cols[1], back_of(rank, 0))
        w2, w3 = weights(cols[2], cols[3], back_of(rank, 0))
        left, right = weights(cols[0] + cols[1], cols[2] + cols[3], back_of(rank, 1))
        return w0 * left, w1 * left, w2 * right, w3 * right

    def over_bc(i):
        for j in range(1, NXC):
            send_x(0, i, j).wait_recv()
        for zo in range(2):
            cols = columns(i, zo)
            w = shares(cols)
            bases = [sbc_v[i, x, zo, 0]] + [rbc_v[i, j, zo, 0] for j in range(3)]
            cbc_v[i, zo, 0] = (w[0] * bases[0] + w[1] * bases[1]) + (w[2] * bases[2] + w[3] * bases[3])
            cbc_v[i, zo, 1] = (cols[0] + cols[1]) + (cols[2] + cols[3])

        @pl.when(i < NB - 1)
        def _():
            send_z(0, i, 0).start()
            send_z(0, i, 1).start()

        @pl.when(i == NB - 1)
        def _():
            send_z(0, i, 1 - zl).start()
            for ch in range(2):
                zbc_v[z, ch] = cbc_v[i, zl, ch]

    def over_l(i):
        for j in range(1, NXC):
            send_x(1, i, j).wait_recv()
        for zo in range(2):
            lits = [sl_v[i, x, zo]] + [rl_v[i, j, zo] for j in range(3)]
            w = shares(columns(i, zo))
            cl_v[i, zo] = (w[0] * lits[0] + w[1] * lits[1]) + (w[2] * lits[2] + w[3] * lits[3])

        @pl.when(i < NB - 1)
        def _():
            send_z(1, i, 0).start()
            send_z(1, i, 1).start()

        @pl.when(i == NB - 1)
        def _():
            send_z(1, i, 1 - zl).start()
            zl_v[z] = cl_v[i, zl]

    pl.semaphore_wait(known_sem.at[2], 2)

    def bc_early(i, carry):
        over_bc(i)
        return carry

    lax.fori_loop(0, EARLY, bc_early, 0)

    def rest(i, carry):
        over_l(i)

        @pl.when(i < NB - EARLY)
        def _():
            over_bc(i + EARLY)

        return carry

    lax.fori_loop(0, NB, rest, 0)

    def bc_in(k, carry):
        from_z(0, k).wait_recv()
        return carry

    lax.fori_loop(1, NZC, bc_in, 0)
    cols = [zbc_v[k, 1] for k in range(NZC)]
    w = [None] * NZC
    bit, size = 2, 1
    while len(cols) > 1:
        back = back_of(order_ref[0], bit)
        joined = []
        for k in range(0, len(cols), 2):
            for part, weight in zip((k, k + 1), weights(cols[k], cols[k + 1], back), strict=True):
                for q in range(part * size, (part + 1) * size):
                    w[q] = weight if w[q] is None else w[q] * weight
            joined.append(cols[k] + cols[k + 1])
        cols = joined
        bit, size = bit + 1, size * 2

    def total(terms):
        while len(terms) > 1:
            terms = [terms[k] + terms[k + 1] for k in range(0, len(terms), 2)]
        return terms[0]

    base = total([w[k] * zbc_v[k, 0] for k in range(NZC)])
    out_ref[3] = cols[0]

    def l_in(k, carry):
        from_z(1, k).wait_recv()
        return carry

    lax.fori_loop(1, NZC, l_in, 0)
    lit = total([w[k] * zl_v[k] for k in range(NZC)]) * source
    for ch in range(3):
        out_ref[ch] = (amb_ref[ch] * (-1.0 / kappa)) * base + (dif_ref[ch] * (-1.0 / kappa)) * lit

    for j in range(1, NXS):
        send_tot(j).wait_send()

    def left_x(i, carry):
        for kind in range(2):
            for j in range(1, NXC):
                send_x(kind, i, j).wait_send()
        return carry

    lax.fori_loop(0, NB, left_x, 0)

    def left_z(i, carry):
        for kind in range(2):
            for zo in range(2):
                send_z(kind, i, zo).wait_send()
        return carry

    lax.fori_loop(0, NB - 1, left_z, 0)
    for kind in range(2):
        send_z(kind, NB - 1, 1 - zl).wait_send()


def on_device(density, clip_flags, band_offset, order, ambient, diffuse):
    hbm = pl.BlockSpec(memory_space=pltpu.HBM)
    dma = pltpu.SemaphoreType.DMA
    flags = jnp.transpose(clip_flags, (1, 2, 0))
    bc = (2, 2, CELLS)
    raw = pl.pallas_call(
        kernel,
        out_shape=jax.ShapeDtypeStruct((4, 2, CELLS), F32),
        in_specs=[hbm] * 6,
        out_specs=pl.BlockSpec(memory_space=pltpu.VMEM),
        scratch_shapes=[
            pltpu.SMEM(order.shape, order.dtype),
            pltpu.SMEM(band_offset.shape, band_offset.dtype),
            pltpu.SMEM(ambient.shape, ambient.dtype),
            pltpu.SMEM(diffuse.shape, diffuse.dtype),
            pltpu.SMEM(flags.shape, flags.dtype),
            pltpu.VMEM((NB, SZ, RB, CELLS), BF16),
            pltpu.VMEM((NB, SZ * RB, CELLS), BF16),
            pltpu.VMEM((CELLS, CELLS // 2), BF16),
            pltpu.VMEM((SZ * RB, CELLS), F32),
            pltpu.VMEM((NB, SZ * RB, CELLS), F32),
            pltpu.VMEM((NB, SZ * RB), F32),
            pltpu.VMEM((NXS, NB, SZ * RB), F32),
            pltpu.VMEM((NB, SZ * RB, XB), F32),
            pltpu.VMEM((NB, NXC, 2) + bc, F32),
            pltpu.VMEM((NB, NXC, 2, 2, CELLS), F32),
            pltpu.VMEM((NB, NXC - 1, 2) + bc, F32),
            pltpu.VMEM((NB, NXC - 1, 2, 2, CELLS), F32),
            pltpu.VMEM((NB, 2) + bc, F32),
            pltpu.VMEM((NB, 2, 2, CELLS), F32),
            pltpu.VMEM((NZC,) + bc, F32),
            pltpu.VMEM((NZC, 2, CELLS), F32),
            dma((5,)), dma((NB,)), dma((NXS,)), dma((NXS,)), dma((2, NB, NXC - 1)), dma((2, NB, NXC - 1)),
            dma((2, NB, 2)), dma((2, NZC)),
            pltpu.SemaphoreType.REGULAR((3,)),
        ],
        compiler_params=pltpu.CompilerParams(collective_id=0, has_side_effects=True, vmem_limit_bytes=63 * 2**20),
    )(order, band_offset, ambient, diffuse, flags, density)
    channel = lax.broadcasted_iota(jnp.int32, raw.shape, 0)
    return jnp.where(channel == 3, -jnp.expm1(raw), raw)


def solution(mesh):
    return jax.shard_map(
        on_device,
        mesh=mesh,
        in_specs=(P("depth", None, "xs"), P("depth", None, "xs"), P(), P(), P(), P()),
        out_specs=P(None, "depth", "xs"),
        check_vma=False,
    )
```

time: 40.9 us -> 36.7 us (0.90)
  Pallas kernels: 38.6 us -> 34.4 us
    pallas_call x1, Pallas kernels: 38.6 us -> 34.4 us  [on_device(): pl.pallas_call(kernel, out_shape=jax.ShapeDtypeStruct((4, 2, CELLS), F32)...]
where the time goes in v3:
time: 36.7 us; the launch traced here: 36.5 us
  Pallas kernels  34.4 us (94%)
  other arithmetic  1.4 us (4%)
  between operations  0.67 us (2%)
    pallas_call x1, Pallas kernels, on_device(): pl.pallas_call(kernel, out_shape=jax.ShapeDtypeStruct((4, 2, CELLS), F32)...  34.4 us
    select_n x1, other arithmetic, on_device(): return jnp.where(channel == 3, -jnp.expm1(raw), raw)  1.4 us

profile of v3, /device:TPU:1, one launch (start us, length us, event | category | flops | bytes accessed | tf_op | source)
XLA Modules:
  0.0 36.5 jit_solution(9115706985268559022)
XLA Ops:
  0.7 34.4 %shard_map.64 = f32[4,2,512]{2,1,0:T(2,128)} custom-call(s32[64]{0:T(128)} %order_hbm.1, s32[1]{0:T(128)S(6)} %copy.7.off_hbm, f32[3]{0:T(128)} %amb_hbm.1, f32[3]{0:T(128)} %dif_hbm.1, s32[8,4,16]{2,1,0:T(4,128)} %bitcast.1, bf16[16,128,512]{2,1,0:T(8,128)(2,1)} %dens_ref.1), custom_call_target="tpu_custom_call" | custom-call | tf_op jit(solution)/shard_map/pallas_call | solution.py:364
  35.1 1.4 %negate_select_fusion = f32[4,2,512]{2,1,0:T(2,128)} fusion(f32[4,2,512]{2,1,0:T(2,128)} %shard_map.64, pred[4]{0:T(512)(128)(4,1)S(1)} %iota_compare_fusion), kind=kLoop, calls=%fused_computation | loop fusion | flops 8192 | bytes 32772 | tf_op jit(solution)/shard_map/jit(_where)/select_n | solution.py:398
  (1 shorter events, 0.0 us)

commit v4 on v3

--- a/solution.py
+++ b/solution.py
@@ -35,8 +35,8 @@
 
 def kernel(
     order_hbm, off_hbm, amb_hbm, dif_hbm, flag_hbm, dens_ref, out_ref,
-    order_ref, off_ref, amb_ref, dif_ref, flag_ref,
-    dens_v, m_v, u_v, l_v, p_v, tot_v, totr_v, e_v, sbc_v, sl_v, rbc_v, rl_v, cbc_v, cl_v, zbc_v, zl_v,
+    order_ref, off_ref, amb_ref, dif_ref, flag_ref, flag_v,
+    dens_v, m_v, u_v, l_v, p_v, pick_v, tot_v, totr_v, sbc_v, sl_v, rbc_v, rl_v, cbc_v, cl_v, zbc_v, zl_v,
     small_sem, load_sem, ts_sem, tr_sem, xs_sem, xr_sem, zs_sem, zr_sem, known_sem,
 ):
     d = lax.axis_index("depth")
@@ -60,7 +60,7 @@
     small = [
         pltpu.make_async_copy(source, target, small_sem.at[k])
         for k, (source, target) in enumerate((
-            (flag_hbm, flag_ref), (order_hbm, order_ref), (off_hbm, off_ref), (amb_hbm, amb_ref), (dif_hbm, dif_ref),
+            (flag_hbm, flag_ref), (flag_hbm, flag_v), (order_hbm, order_ref), (off_hbm, off_ref), (amb_hbm, amb_ref), (dif_hbm, dif_ref),
         ))
     ]
 
@@ -97,6 +97,7 @@
         )
 
     small[0].start()
+    small[1].start()
     for i in range(NB):
         load(i).start()
     barrier = pltpu.get_barrier_semaphore()
@@ -106,7 +107,7 @@
         pl.semaphore_signal(barrier, inc=1, device_id=at(z, xor(x, j, 2)), device_id_type=MESH)
     for step in (1, NZC - 1):
         pl.semaphore_signal(barrier, inc=1, device_id=at((z + step) % NZC, x), device_id_type=MESH)
-    for copy in small[1:]:
+    for copy in small[2:]:
         copy.start()
 
     def tell(k):
@@ -122,34 +123,46 @@
         lax.broadcasted_iota(jnp.int32, (wide, wide), 0) < lax.broadcasted_iota(jnp.int32, (wide, wide), 1), ratio, 0.0
     ).astype(BF16)
 
+    blocks = CELLS // XB
+    for i in range(NB):
+        for c in range(blocks):
+            column = lax.broadcasted_iota(jnp.int32, (XB, XB), 1) == blocks * i + c
+            pick_v[i, c * XB:(c + 1) * XB, :] = jnp.where(column, -kappa * ratio, 0.0).astype(BF16)
+    spread = (
+        lax.broadcasted_iota(jnp.int32, (SZ, SZ * RB), 1) // RB == lax.broadcasted_iota(jnp.int32, (SZ, SZ * RB), 0)
+    ).astype(BF16)
+
+    small[0].wait()
+    small[1].wait()
+
+    kept = [
+        jnp.dot(flag_v[block_of(i)].astype(F32).astype(BF16), spread, preferred_element_type=F32) for i in range(NB)
+    ]
+    sums = jnp.zeros((SZ * RB, XB), F32)
+    for i in range(NB):
+        load(i).wait()
+        sums = sums + jnp.dot(
+            dens_v[i].reshape(SZ * RB, CELLS), pick_v[i], preferred_element_type=F32
+        )
+    sums = sums.T
+    for i in range(NB):
+        tot_v[i:i + 1, :] = jnp.sum(sums[blocks * i:blocks * (i + 1), :] * kept[i], axis=0, keepdims=True)
     pl.semaphore_wait(barrier, NXS - 1 + NXC - 1 + 2)
     tell(0)
-
-    small[0].wait()
-
-    def clip(i, carry):
-        load(i).wait()
+    for j in range(1, NXS):
+        send_tot(j).start()
+
+    def clip(i):
         b = block_of(i)
         for q in range(SZ):
             for c in range(CELLS // XB):
                 scale = flag_ref[b, c, q].astype(F32) * (-kappa)
                 cells = slice(c * XB, (c + 1) * XB)
-                m_v[i, q * RB:(q + 1) * RB, cells] = (dens_v[i, q, :, cells].astype(F32) * scale).astype(BF16)
-        return carry
-
-    lax.fori_loop(0, NB, clip, 0)
-
-    ones = jnp.full((8, CELLS), ratio, BF16)
-    for i in range(NB):
-        sums = lax.dot_general(ones, m_v[i], (((1,), (1,)), ((), ())), preferred_element_type=F32)
-        tot_v[i:i + 1, :] = sums[0:1, :]
-    for j in range(1, NXS):
-        send_tot(j).start()
-    pl.semaphore_wait(known_sem.at[0], 2)
-    tell(1)
+                m_v[q * RB:(q + 1) * RB, cells] = (dens_v[i, q, :, cells].astype(F32) * scale).astype(BF16)
 
     def local(i):
-        m = m_v[i]
+        clip(i)
+        m = m_v[...]
         l_v[:, 0:wide] = jnp.dot(m[:, 0:wide], u_v[wide:, :], preferred_element_type=F32)
         l_v[:, wide:] = jnp.dot(m, u_v[...], preferred_element_type=F32)
         for h in range(2):
@@ -159,7 +172,7 @@
             clear = jnp.ones((RB, wide), F32)
             for q in range(SZ):
                 rows = slice(q * RB, (q + 1) * RB)
-                y = m_v[i, rows, lanes].astype(F32)
+                y = m_v[rows, lanes].astype(F32)
                 depth = depth + y
                 behind = jnp.exp(depth)
                 term = y * (clear - behind)
@@ -170,15 +183,23 @@
                 sbc_v[i, g % 4, g // 4, 0, :, lanes] = base[2 * g:2 * g + 2, :]
                 sbc_v[i, g % 4, g // 4, 1, :, lanes] = depth[2 * g:2 * g + 2, :]
 
+    def send_bc(i):
+        for j in range(1, NXC):
+            send_x(0, i, j).start()
+
     def produce(i, carry):
         local(i)
 
         @pl.when(i < EARLY)
         def _():
-            for j in range(1, NXC):
-                send_x(0, i, j).start()
-
-        @pl.when(i == NB // 2)
+            send_bc(i)
+
+        @pl.when(i == 1)
+        def _():
+            pl.semaphore_wait(known_sem.at[0], 2)
+            tell(1)
+
+        @pl.when(i == 4)
         def _():
             pl.semaphore_wait(known_sem.at[1], 2)
             tell(2)
@@ -187,7 +208,7 @@
 
     lax.fori_loop(0, NB, produce, 0)
 
-    for copy in small[1:]:
+    for copy in small[2:]:
         copy.wait()
     row = lax.broadcasted_iota(jnp.int32, (2, CELLS), 0) + (2 * d + off_ref[0])
     source = 0.6 + 0.4 * jnp.cos((row % 64).astype(F32) * (2.0 * math.pi / 64.0))
@@ -198,14 +219,12 @@
     for j in range(1, NXS):
         nearer = nearer + totr_v[j] * (xor(s, j, 3) < s).astype(F32)
     factor = jnp.exp(nearer).T
-    for i in range(NB):
-        e_v[i] = jnp.broadcast_to(factor[:, i:i + 1], (SZ * RB, XB))
-
-    def shade(i, carry):
+
+    def shade(i):
         lit = [jnp.zeros((RB, XB), F32)] * (CELLS // XB)
         for q in range(SZ):
             rows = slice(q * RB, (q + 1) * RB)
-            e = e_v[i, rows, :]
+            e = jnp.broadcast_to(factor[rows, i:i + 1], (RB, XB))
             for c in range(CELLS // XB):
                 lit[c] = lit[c] + p_v[i, rows, c * XB:(c + 1) * XB] * e
         for c in range(CELLS // XB):
@@ -214,14 +233,10 @@
         for j in range(1, NXC):
             send_x(1, i, j).start()
 
-        @pl.when(i < NB - EARLY)
-        def _():
-            for j in range(1, NXC):
-                send_x(0, i + EARLY, j).start()
-
-        return carry
-
-    lax.fori_loop(0, NB, shade, 0)
+    for i in range(NB):
+        shade(i)
+        if i + EARLY < NB:
+            send_bc(i + EARLY)
 
     def back_of(rank, bit):
         return ((rank // 2**bit) % 2).astype(F32)
@@ -323,7 +338,11 @@
         return terms[0]
 
     base = total([w[k] * zbc_v[k, 0] for k in range(NZC)])
-    out_ref[3] = cols[0]
+    col = cols[0]
+    series = 1.0 + col * (1.0 / 6.0)
+    for k in (5, 4, 3, 2):
+        series = 1.0 + col * (1.0 / k) * series
+    out_ref[3] = jnp.where(col > -0.125, -col * series, 1.0 - jnp.exp(col))
 
     def l_in(k, carry):
         from_z(1, k).wait_recv()
@@ -361,7 +380,7 @@
     dma = pltpu.SemaphoreType.DMA
     flags = jnp.transpose(clip_flags, (1, 2, 0))
     bc = (2, 2, CELLS)
-    raw = pl.pallas_call(
+    return pl.pallas_call(
         kernel,
         out_shape=jax.ShapeDtypeStruct((4, 2, CELLS), F32),
         in_specs=[hbm] * 6,
@@ -372,14 +391,15 @@
             pltpu.SMEM(ambient.shape, ambient.dtype),
             pltpu.SMEM(diffuse.shape, diffuse.dtype),
             pltpu.SMEM(flags.shape, flags.dtype),
+            pltpu.VMEM(flags.shape, flags.dtype),
             pltpu.VMEM((NB, SZ, RB, CELLS), BF16),
-            pltpu.VMEM((NB, SZ * RB, CELLS), BF16),
+            pltpu.VMEM((SZ * RB, CELLS), BF16),
             pltpu.VMEM((CELLS, CELLS // 2), BF16),
             pltpu.VMEM((SZ * RB, CELLS), F32),
             pltpu.VMEM((NB, SZ * RB, CELLS), F32),
+            pltpu.VMEM((NB, CELLS, XB), BF16),
             pltpu.VMEM((NB, SZ * RB), F32),
             pltpu.VMEM((NXS, NB, SZ * RB), F32),
-            pltpu.VMEM((NB, SZ * RB, XB), F32),
             pltpu.VMEM((NB, NXC, 2) + bc, F32),
             pltpu.VMEM((NB, NXC, 2, 2, CELLS), F32),
             pltpu.VMEM((NB, NXC - 1, 2) + bc, F32),
@@ -388,14 +408,12 @@
             pltpu.VMEM((NB, 2, 2, CELLS), F32),
             pltpu.VMEM((NZC,) + bc, F32),
             pltpu.VMEM((NZC, 2, CELLS), F32),
-            dma((5,)), dma((NB,)), dma((NXS,)), dma((NXS,)), dma((2, NB, NXC - 1)), dma((2, NB, NXC - 1)),
+            dma((6,)), dma((NB,)), dma((NXS,)), dma((NXS,)), dma((2, NB, NXC - 1)), dma((2, NB, NXC - 1)),
             dma((2, NB, 2)), dma((2, NZC)),
             pltpu.SemaphoreType.REGULAR((3,)),
         ],
         compiler_params=pltpu.CompilerParams(collective_id=0, has_side_effects=True, vmem_limit_bytes=63 * 2**20),
     )(order, band_offset, ambient, diffuse, flags, density)
-    channel = lax.broadcasted_iota(jnp.int32, raw.shape, 0)
-    return jnp.where(channel == 3, -jnp.expm1(raw), raw)
 
 
 def solution(mesh):

time: 36.7 us -> 35.3 us (0.962); the launches traced: 36.5 us -> 34.7 us
  Pallas kernels: 34.4 us -> 32.7 us
  other arithmetic: 1.4 us -> 0 us
  local copies, waits for them, and re-layouts: 0 us -> 1.32 us
    pallas_call x1, Pallas kernels: 34.4 us -> 32.7 us  [on_device(): pl.pallas_call(kernel, out_shape=jax.ShapeDtypeStruct((4, 2, CELLS), F32)...]
    select_n x1 -> x0, other arithmetic: 1.4 us -> none  [on_device(): return jnp.where(channel == 3, -jnp.expm1(raw), raw)]
    unnamed x0 -> x1, local copies, waits for them, and re-layouts: none -> 1.32 us
where the time goes in v4:
time: 35.3 us; the launch traced here: 34.7 us
  Pallas kernels  32.7 us (93%)
  local copies, waits for them, and re-layouts  1.32 us (4%)
  between operations  0.66 us (2%)
    pallas_call x1, Pallas kernels, on_device(): pl.pallas_call(kernel, out_shape=jax.ShapeDtypeStruct((4, 2, CELLS), F32)...  32.7 us
    unnamed x1, local copies, waits for them, and re-layouts  1.32 us

profile of v4, /device:TPU:1, one launch (start us, length us, event | category | flops | bytes accessed | tf_op | source)
XLA Modules:
  0.0 34.7 jit_solution(12188570113099707575)
XLA Ops:
  0.7 32.7 %shard_map.64 = f32[4,2,512]{2,1,0:T(2,128)} custom-call(s32[64]{0:T(128)} %order_hbm.1, s32[1]{0:T(128)S(6)} %copy.8.off_hbm, f32[3]{0:T(128)} %amb_hbm.1, f32[3]{0:T(128)} %dif_hbm.1, s32[8,4,16]{2,1,0:T(4,128)} %bitcast.1, bf16[16,128,512]{2,1,0:T(8,128)(2,1)} %dens_ref.1), custom_call_target="tpu_custom_call" | custom-call | tf_op jit(solution)/shard_map/pallas_call | solution.py:383
  33.4 1.3 %copy.9 = f32[4,2,512]{2,1,0:T(2,128)} copy(f32[4,2,512]{2,1,0:T(2,128)} %shard_map.64) | data formatting | bytes 32768

commit v5 on v4

--- a/solution.py
+++ b/solution.py
@@ -96,10 +96,6 @@
             device_id=at(peer, x), device_id_type=MESH,
         )
 
-    small[0].start()
-    small[1].start()
-    for i in range(NB):
-        load(i).start()
     barrier = pltpu.get_barrier_semaphore()
     for j in range(1, NXS):
         pl.semaphore_signal(barrier, inc=1, device_id=(d, xor(s, j, 3)), device_id_type=MESH)
@@ -107,6 +103,10 @@
         pl.semaphore_signal(barrier, inc=1, device_id=at(z, xor(x, j, 2)), device_id_type=MESH)
     for step in (1, NZC - 1):
         pl.semaphore_signal(barrier, inc=1, device_id=at((z + step) % NZC, x), device_id_type=MESH)
+    small[0].start()
+    small[1].start()
+    for i in range(NB):
+        load(i).start()
     for copy in small[2:]:
         copy.start()
 

time: 35.3 us -> 35.2 us (level)
  no operation moved by 1% of the time
where the time goes in v5:
time: 35.2 us; the launch traced here: 34.7 us
  Pallas kernels  32.7 us (93%)
  local copies, waits for them, and re-layouts  1.32 us (4%)
  between operations  0.66 us (2%)
    pallas_call x1, Pallas kernels, on_device(): pl.pallas_call(kernel, out_shape=jax.ShapeDtypeStruct((4, 2, CELLS), F32)...  32.7 us
    unnamed x1, local copies, waits for them, and re-layouts  1.32 us

profile of v5, /device:TPU:1, one launch (start us, length us, event | category | flops | bytes accessed | tf_op | source)
XLA Modules:
  0.0 34.7 jit_solution(1792090976905901508)
XLA Ops:
  0.7 32.7 %shard_map.64 = f32[4,2,512]{2,1,0:T(2,128)} custom-call(s32[64]{0:T(128)} %order_hbm.1, s32[1]{0:T(128)S(6)} %copy.8.off_hbm, f32[3]{0:T(128)} %amb_hbm.1, f32[3]{0:T(128)} %dif_hbm.1, s32[8,4,16]{2,1,0:T(4,128)} %bitcast.1, bf16[16,128,512]{2,1,0:T(8,128)(2,1)} %dens_ref.1), custom_call_target="tpu_custom_call" | custom-call | tf_op jit(solution)/shard_map/pallas_call | solution.py:383
  33.4 1.3 %copy.9 = f32[4,2,512]{2,1,0:T(2,128)} copy(f32[4,2,512]{2,1,0:T(2,128)} %shard_map.64) | data formatting | bytes 32768
